TPU v7x, 512 devices: a whole 4x4x16 slice. The times are simulated.
512 devices in a mesh: tm: 32 (over z, core), bat: 16 (over y, x).
Axes of the slice: x: 4, y: 4, z: 16, core: 2. Of those that a mesh axis runs over, the one named last changes fastest.
Arguments:
- power0: float32 [512, 6144], P('tm', 'bat'), may hold values from -0.5 to 0.5
- charge0: float32 [512, 6144], P('tm', 'bat'), may hold values from 0 to 1
- dyn_dual0: float32 [512, 6144], P('tm', 'bat'), may hold values from -3 to 3
- feeder_dual0: float32 [512, 3072], P(('tm', 'bat')), may hold values from 0 to 0.5
- price: float32 [512, 6144], P('tm', 'bat'), may hold values from -12 to 12
- inflow: float32 [512, 6144], P('tm', 'bat'), may hold values from -1.5 to 1.5
- power_limit: float32 [6144], P('bat'), may hold values from 0.5 to 6
- capacity: float32 [6144], P('bat'), may hold values from 0.5 to 8
- feeder_limit: float32 [3072], replicated, may hold values from 0 to 1
- block_values: float32 [72, 128, 128], replicated, may hold values from -0.3125 to 0.3125
- block_cols: int32 [72], replicated, may hold values from 0 to 47, as said below
- block_offsets: int32 [25], replicated, may hold values from 0 to 72, as said below
Outputs:
- power: float32 [512, 6144], P('tm', 'bat')
- charge: float32 [512, 6144], P('tm', 'bat')
- dyn_dual: float32 [512, 6144], P('tm', 'bat')
- feeder_dual: float32 [512, 3072], P(('tm', 'bat'))
Inputs may be any that keep to these rules, and one draw needn't show every extreme that they name: `block_cols`: every battery block 0 to 47 appears at least once. block_offsets[0] = 0, strictly rising, block_offsets[24] = 72.
All inputs are finite; a program needn't handle non-finite values.
Results may differ from a plain program's by a relative error of at most 0.0001.
Values sent between devices are 32-bit elements; how exact they have to be, the bound alone decides.
No kernel may reach another device: no remote copies, remote signals or barrier semaphores. Data moves between devices by JAX's collectives and lax.ppermute only.
A program may use at most 64 MiB of HBM per device.

v0:
```python
import jax
import jax.numpy as jnp
from jax import lax
from jax.sharding import PartitionSpec as P

ITERS = 4
HIGH = lax.Precision.HIGHEST
ETA_STEP = 0.4
EPS_NORM = 1e-06


def shifted(block, axis, distance):
    devices = range(lax.axis_size(axis))
    route = [(i - distance, i) for i in devices if i - distance in devices]
    return lax.ppermute(block, axis, route)


def row_table(block_offsets, count):
    index_all = jnp.arange(count, dtype=jnp.int32)
    row_of = jnp.sum((index_all[:, None] >= block_offsets[None, 1:-1]).astype(jnp.int32), axis=1)
    feed_count = block_offsets.shape[0] - 1
    return (row_of[:, None] == jnp.arange(feed_count, dtype=jnp.int32)[None, :]).astype(jnp.float32)


def feeder_apply(field, block_values, rows_tab, cols_tab):
    count_rows = field.shape[0]
    blk = block_values.shape[1]
    blocks = field.reshape(count_rows, -1, blk)
    picked = jnp.einsum("rnk,jn->rjk", blocks, cols_tab, precision=HIGH)
    partial_rows = jnp.einsum("rjk,jmk->rjm", picked, block_values, precision=HIGH)
    summed = jnp.einsum("rjm,jf->rfm", partial_rows, rows_tab, precision=HIGH)
    return summed.reshape(count_rows, -1)


def feeder_adjoint(duals, block_values, rows_tab, cols_tab):
    count_rows = duals.shape[0]
    blk = block_values.shape[1]
    blocks = duals.reshape(count_rows, -1, blk)
    chosen = jnp.einsum("rfm,jf->rjm", blocks, rows_tab, precision=HIGH)
    pushed = jnp.einsum("rjm,jmk->rjk", chosen, block_values, precision=HIGH)
    spread = jnp.einsum("rjk,jn->rnk", pushed, cols_tab, precision=HIGH)
    return spread.reshape(count_rows, -1)


def shards(
    power0,
    charge0,
    dyn_dual0,
    feeder_dual0,
    price,
    inflow,
    power_limit,
    capacity,
    feeder_limit,
    block_values,
    block_cols,
    block_offsets,
):
    blk = block_values.shape[1]
    rows_tab = row_table(block_offsets, block_values.shape[0])
    local_batteries = power0.shape[1]
    local_blocks = local_batteries // blk
    first_block = lax.axis_index("bat") * local_blocks
    inside = (block_cols >= first_block) & (block_cols < first_block + local_blocks)
    local_cols = jnp.clip(block_cols - first_block, 0, local_blocks - 1)
    local_tab = (
        (local_cols[:, None] == jnp.arange(local_blocks, dtype=jnp.int32)[None, :])
        & inside[:, None]
    ).astype(jnp.float32)

    def couple_backward(duals):
        return feeder_adjoint(
            lax.all_gather(duals, "bat", axis=0, tiled=True), block_values, rows_tab, local_tab
        )

    power, charge, dyn_dual, feeder_dual = (power0, charge0, dyn_dual0, feeder_dual0)
    weight = jnp.asarray(1.0, dtype=jnp.float32)
    pushed = couple_backward(feeder_dual)
    limit_row = power_limit[None, :]
    for iteration in range(ITERS):
        step_primal = ETA_STEP / weight
        step_dual = ETA_STEP * weight
        following = shifted(dyn_dual[:1], "tm", -1)
        dual_next = jnp.concatenate([dyn_dual[1:], following], axis=0)
        power_new = jnp.clip(
            power - step_primal * (price - dyn_dual + pushed), -limit_row, limit_row
        )
        charge_new = jnp.clip(charge - step_primal * (dyn_dual - dual_next), 0.0, capacity[None, :])
        power_bar = 2.0 * power_new - power
        charge_bar = 2.0 * charge_new - charge
        last_iteration = iteration + 1 == ITERS
        if not last_iteration:
            move_power = power_new - power
            move_charge = charge_new - charge
            primal_local = jnp.sum(move_power * move_power + move_charge * move_charge)
            primal_sq = lax.psum(primal_local, ("tm", "bat"))
        coupled = lax.psum_scatter(
            feeder_apply(power_bar, block_values, rows_tab, local_tab),
            "bat",
            scatter_dimension=0,
            tiled=True,
        )
        preceding = shifted(charge_bar[-1:], "tm", 1)
        charge_prev = jnp.concatenate([preceding, charge_bar[:-1]], axis=0)
        dyn_new = dyn_dual + step_dual * (charge_bar - charge_prev - power_bar - inflow)
        feeder_new = jnp.maximum(0.0, feeder_dual + step_dual * (coupled - feeder_limit[None, :]))
        if not last_iteration:
            move_dyn = dyn_new - dyn_dual
            move_feed = feeder_new - feeder_dual
            dual_local = jnp.sum(move_dyn * move_dyn) + jnp.sum(move_feed * move_feed)
            dual_sq = lax.psum(dual_local, ("tm", "bat"))
            weight = jnp.sqrt(weight * jnp.sqrt((dual_sq + EPS_NORM) / (primal_sq + EPS_NORM)))
            pushed = couple_backward(feeder_new)
        power, charge, dyn_dual, feeder_dual = (power_new, charge_new, dyn_new, feeder_new)
    return (power, charge, dyn_dual, feeder_dual)


def solution(mesh):
    return jax.shard_map(
        shards,
        mesh=mesh,
        in_specs=(
            P("tm", "bat"),
            P("tm", "bat"),
            P("tm", "bat"),
            P(("tm", "bat"), None),
            P("tm", "bat"),
            P("tm", "bat"),
            P("bat"),
            P("bat"),
            P(),
            P(),
            P(),
            P(),
        ),
        out_specs=(P("tm", "bat"), P("tm", "bat"), P("tm", "bat"), P(("tm", "bat"), None)),
        check_vma=False,
    )
```

profile of v0, /device:TPU:2, one launch (start us, length us, event | category | flops | bytes accessed | tf_op | source)
XLA Modules:
  0.0 976.7 jit_solution(11067665464385182962)
XLA Ops:
  7.3 0.7 slice.53
  8.0 1.3 collective-permute-start
  9.3 0.7 subtract_clamp_fusion
  9.9 0.7 compare_and_fusion
  10.6 0.7 slice.51
  11.4 26.6 %all-gather = f32[16,1,3072]{2,1,0:T(1,128)S(1)} all-gather(f32[1,1,3072]{2,1,0:T(1,128)} %bitcast.181), channel_id=1, replica_groups=mesh['tm'=32,'bat'=16] {'bat'}, dimensions={0}, use_global_device_ids=true | all-gather | bytes 208896 | tf_op jit(solution)/shard_map/all_gather | solution.py:73
  38.5 5.8 convolution_bitcast_fusion.15
  44.9 0.6 add_reduce_fusion.2
  45.5 1.3 collective-permute-start.1
  46.8 0.8 collective-permute-done.1
  48.7 9.2 convolution_bitcast_fusion.14
  58.4 0.7 copy.103
  59.2 1.3 dynamic-slice
  60.5 1.3 collective-permute-start.2
  61.8 115.7 %all-reduce.12.cloned.1.call-done = f32[16,3072]{1,0:T(8,128)} async-done(((f32[16,3072]{1,0:T(8,128)}), f32[16,3072]{1,0:T(8,128)}) %all-reduce.12.cloned.1.call-update) | async-done | bytes 196624
  177.5 2.2 multiply_reduce_fusion.5
  179.7 22.0 %all-gather.1 = f32[16,1,3072]{2,1,0:T(1,128)S(1)} all-gather(f32[1,1,3072]{2,1,0:T(1,128)S(1)} %bitcast.179), channel_id=1, replica_groups=mesh['tm'=32,'bat'=16] {'bat'}, dimensions={0}, use_global_device_ids=true | all-gather | bytes 208896 | tf_op jit(solution)/shard_map/all_gather | solution.py:73
  202.1 5.8 convolution_bitcast_fusion.13
  209.7 103.0 %all-reduce.6 = (f32[]{:T(128)}, f32[]{:T(128)}) all-reduce(f32[]{:T(128)S(6)} %add.99, f32[]{:T(128)} %get-tuple-element.31), channel_id=1, replica_groups=mesh['tm'=32,'bat'=16] {'tm','bat'}, use_global_device_ids=true, to_apply=%region_4.5 | all-reduce | flops 2 | bytes 16 | tf_op jit(solution)/shard_map/psum | solution.py:111
  314.2 0.6 add_reduce_fusion.1
  314.8 1.9 collective-permute-start.3
  316.8 0.6 collective-permute-done.3
  318.5 9.2 convolution_bitcast_fusion.12
  328.1 0.7 copy.102
  329.0 1.3 collective-permute-start.4
  330.3 110.9 %all-reduce.14.cloned.1.call-done = f32[16,3072]{1,0:T(8,128)} async-done(((f32[16,3072]{1,0:T(8,128)}), f32[16,3072]{1,0:T(8,128)}) %all-reduce.14.cloned.1.call-update) | async-done | bytes 196624
  441.1 2.2 multiply_reduce_fusion.4
  443.3 22.0 %all-gather.2 = f32[16,1,3072]{2,1,0:T(1,128)S(1)} all-gather(f32[1,1,3072]{2,1,0:T(1,128)S(1)} %bitcast.178), channel_id=1, replica_groups=mesh['tm'=32,'bat'=16] {'bat'}, dimensions={0}, use_global_device_ids=true | all-gather | bytes 208896 | tf_op jit(solution)/shard_map/all_gather | solution.py:73
  465.7 5.8 convolution_bitcast_fusion.11
  473.3 103.0 %all-reduce.5 = (f32[]{:T(128)}, f32[]{:T(128)}) all-reduce(f32[]{:T(128)S(6)} %add.106, f32[]{:T(128)} %get-tuple-element.23), channel_id=1, replica_groups=mesh['tm'=32,'bat'=16] {'tm','bat'}, use_global_device_ids=true, to_apply=%region_10.11 | all-reduce | flops 2 | bytes 16 | tf_op jit(solution)/shard_map/psum | solution.py:111
  577.8 0.6 add_reduce_fusion
  578.4 1.7 collective-permute-start.5
  580.2 0.8 collective-permute-done.5
  582.1 9.2 convolution_bitcast_fusion.10
  591.7 0.7 copy.101
  592.5 1.3 collective-permute-start.6
  593.8 110.9 %all-reduce.16.cloned.1.call-done = f32[16,3072]{1,0:T(8,128)} async-done(((f32[16,3072]{1,0:T(8,128)}), f32[16,3072]{1,0:T(8,128)}) %all-reduce.16.cloned.1.call-update) | async-done | bytes 196624
  704.7 2.2 multiply_reduce_fusion.3
  706.9 22.2 %all-gather.3 = f32[16,1,3072]{2,1,0:T(1,128)S(1)} all-gather(f32[1,1,3072]{2,1,0:T(1,128)S(1)} %bitcast.180), channel_id=1, replica_groups=mesh['tm'=32,'bat'=16] {'bat'}, dimensions={0}, use_global_device_ids=true | all-gather | bytes 208896 | tf_op jit(solution)/shard_map/all_gather | solution.py:73
  729.5 5.8 convolution_bitcast_fusion.9
  736.7 103.0 %all-reduce.4 = (f32[]{:T(128)}, f32[]{:T(128)}) all-reduce(f32[]{:T(128)S(6)} %add.113, f32[]{:T(128)} %get-tuple-element.15), channel_id=1, replica_groups=mesh['tm'=32,'bat'=16] {'tm','bat'}, use_global_device_ids=true, to_apply=%region_16.17 | all-reduce | flops 2 | bytes 16 | tf_op jit(solution)/shard_map/psum | solution.py:111
  841.1 0.6 multiply_subtract_fusion.1
  841.8 1.7 collective-permute-start.7
  844.3 0.6 fusion.71
  845.4 9.2 convolution_bitcast_fusion.8
  855.1 0.7 copy.100
  855.8 112.2 %all-reduce.18.cloned.1.call-done = f32[16,3072]{1,0:T(8,128)} async-done(((f32[16,3072]{1,0:T(8,128)}), f32[16,3072]{1,0:T(8,128)}) %all-reduce.18.cloned.1.call-update) | async-done | bytes 196624
  968.0 2.1 fusion.92
  (71 shorter events, 9.9 us)
Async XLA Ops:
  7.2 37.6 %copy-start.2 = (f32[16,384]{1,0:T(8,128)S(1)}, f32[16,384]{1,0:T(8,128)}, u32[]{:S(2)}) copy-start(f32[16,384]{1,0:T(8,128)} %param.14) | copy-start | bytes 73732
  7.2 37.6 %copy-start.6 = (f32[384]{0:T(512)S(1)}, f32[384]{0:T(512)}, u32[]{:S(2)}) copy-start(f32[384]{0:T(512)} %param.18) | copy-start | bytes 4612
  7.2 37.6 %copy-start.4 = (f32[16,384]{1,0:T(8,128)S(1)}, f32[16,384]{1,0:T(8,128)}, u32[]{:S(2)}) copy-start(f32[16,384]{1,0:T(8,128)} %param.12) | copy-start | bytes 73732
  7.2 37.6 %copy-start.5 = (f32[16,384]{1,0:T(8,128)S(1)}, f32[16,384]{1,0:T(8,128)}, u32[]{:S(2)}) copy-start(f32[16,384]{1,0:T(8,128)} %param.13) | copy-start | bytes 73732
  7.2 37.6 %copy-start.1 = (f32[16,384]{1,0:T(8,128)S(1)}, f32[16,384]{1,0:T(8,128)}, u32[]{:S(2)}) copy-start(f32[16,384]{1,0:T(8,128)} %param.16) | copy-start | bytes 73732
  7.2 37.6 %copy-start.8 = (f32[384]{0:T(512)S(1)}, f32[384]{0:T(512)}, u32[]{:S(2)}) copy-start(f32[384]{0:T(512)} %param.19) | copy-start | bytes 4612
  7.2 40.4 %copy-start = (f32[16,384]{1,0:T(8,128)S(1)}, f32[16,384]{1,0:T(8,128)}, u32[]{:S(2)}) copy-start(f32[16,384]{1,0:T(8,128)} %param.17) | copy-start | bytes 73732
  7.2 170.3 %all-reduce.12.cloned.1.call-start = ((), (), s32[]{:S(2)}) async-start(), calls=%async_computation | async-start | bytes 393216
  8.0 36.8 %collective-permute-start = (f32[1,384]{1,0:T(1,128)S(1)}, f32[1,384]{1,0:T(1,128)S(1)}, u32[]{:S(2)}, u32[]{:S(2)}) collective-permute-start(f32[1,384]{1,0:T(1,128)S(1)} %slice.53), channel_id=1, source_target_pairs={{16,0},{32,16},{48,32},{64,48},{80,64},{96,80},{112,96},{128,112},... | collective-permute-start | bytes 4616 | tf_op jit(solution)/shard_map/ppermute | solution.py:15
  44.3 133.2 %copy-start.3 = (f32[3072]{0:T(1024)S(1)}, f32[3072]{0:T(1024)}, u32[]{:S(2)}) copy-start(f32[3072]{0:T(1024)} %param.20) | copy-start | bytes 36868
  44.3 133.2 %copy-start.7 = (f32[1,3072]{1,0:T(1,128)S(1)}, f32[1,3072]{1,0:T(1,128)}, u32[]{:S(2)}) copy-start(f32[1,3072]{1,0:T(1,128)} %param.15) | copy-start | bytes 36868
  45.5 2.1 collective-permute-start.1
  59.1 382.0 %all-reduce.14.cloned.1.call-start = ((), (), s32[]{:S(2)}) async-start(), calls=%async_computation.1 | async-start | bytes 393216
  60.5 253.7 %collective-permute-start.2 = (f32[1,384]{1,0:T(1,128)S(1)}, f32[1,384]{1,0:T(1,128)S(1)}, u32[]{:S(2)}, u32[]{:S(2)}) collective-permute-start(f32[1,384]{1,0:T(1,128)S(1)} %slice.71), channel_id=1, source_target_pairs={{16,0},{32,16},{48,32},{64,48},{80,64},{96,80},{112,96},{128,112},... | collective-permute-start | bytes 4616 | tf_op jit(solution)/shard_map/ppermute | solution.py:15
  314.8 2.5 collective-permute-start.3
  328.9 375.8 %all-reduce.16.cloned.1.call-start = ((), (), s32[]{:S(2)}) async-start(), calls=%async_computation.2 | async-start | bytes 393216
  329.0 248.8 %collective-permute-start.4 = (f32[1,384]{1,0:T(1,128)S(1)}, f32[1,384]{1,0:T(1,128)S(1)}, u32[]{:S(2)}, u32[]{:S(2)}) collective-permute-start(f32[1,384]{1,0:T(1,128)S(1)} %slice.75), channel_id=1, source_target_pairs={{16,0},{32,16},{48,32},{64,48},{80,64},{96,80},{112,96},{128,112},... | collective-permute-start | bytes 4616 | tf_op jit(solution)/shard_map/ppermute | solution.py:15
  578.4 2.5 collective-permute-start.5
  592.5 375.6 %all-reduce.18.cloned.1.call-start = ((), (), s32[]{:S(2)}) async-start(), calls=%async_computation.3 | async-start | bytes 393216
  592.5 248.6 %collective-permute-start.6 = (f32[1,384]{1,0:T(1,128)S(1)}, f32[1,384]{1,0:T(1,128)S(1)}, u32[]{:S(2)}, u32[]{:S(2)}) collective-permute-start(f32[1,384]{1,0:T(1,128)S(1)} %slice.79), channel_id=1, source_target_pairs={{16,0},{32,16},{48,32},{64,48},{80,64},{96,80},{112,96},{128,112},... | collective-permute-start | bytes 4616 | tf_op jit(solution)/shard_map/ppermute | solution.py:15
  841.8 2.5 collective-permute-start.7
Sparse Core Ops, SparseCore 0:
  59.2 118.2 all-reduce.11
  329.0 112.0 all-reduce.13
  592.6 112.0 all-reduce.15
  855.9 112.0 all-reduce.17
where the time goes:
time: 978 us; the launch traced here: 977 us
  waiting for transfers between devices  452 us (46%)
  blocking collectives  402 us (41%)
  matrix products  67.2 us (7%)
  between operations  22.5 us (2%)
  other arithmetic  15.1 us (2%)
  starting transfers between devices  12 us (1%)
    unnamed x8, waiting for transfers between devices  450 us
    psum x3, blocking collectives, shards(): dual_sq = lax.psum(dual_local, ('tm', 'bat'))  309 us
    all_gather x4, blocking collectives, couple_backward(): lax.all_gather(duals, 'bat', axis=0, tiled=True)  92.9 us
    dot_general x4, matrix products, feeder_apply(): jnp.einsum('rjk,jmk->rjm', picked, block_values, precision=HIGH)  36.7 us
    dot_general x4, matrix products, feeder_adjoint(): pushed = jnp.einsum('rjm,jmk->rjk', chosen, block_values, precision=HIGH)  23.3 us
  transfers between devices with their start and end apart: 12, of which 8 were waited for; matrix products, arithmetic and copies ran while one was open for 4% of the time, Pallas kernels for 0%

commit v1 on v0

--- a/solution.py
+++ b/solution.py
@@ -7,6 +7,11 @@
 HIGH = lax.Precision.HIGHEST
 ETA_STEP = 0.4
 EPS_NORM = 1e-06
+
+
+def tiled_gather(array, axis, dim):
+    copies = jnp.concatenate([array] * lax.axis_size(axis), axis=dim)
+    return lax.all_to_all(copies, axis, dim, dim, tiled=True)
 
 
 def shifted(block, axis, distance):
@@ -69,9 +74,7 @@
     ).astype(jnp.float32)
 
     def couple_backward(duals):
-        return feeder_adjoint(
-            lax.all_gather(duals, "bat", axis=0, tiled=True), block_values, rows_tab, local_tab
-        )
+        return feeder_adjoint(tiled_gather(duals, "bat", 0), block_values, rows_tab, local_tab)
 
     power, charge, dyn_dual, feeder_dual = (power0, charge0, dyn_dual0, feeder_dual0)
     weight = jnp.asarray(1.0, dtype=jnp.float32)

time: 978 us -> 930 us (0.951)
  blocking collectives: 402 us -> 313 us
  starting transfers between devices: 12 us -> 39 us
    all_gather x4 -> x0, blocking collectives: 92.9 us -> none  [couple_backward(): lax.all_gather(duals, 'bat', axis=0, tiled=True)]
    all_to_all x0 -> x4, starting transfers between devices: none -> 27.2 us  [tiled_gather(): return lax.all_to_all(copies, axis, dim, dim, tiled=True)]
  transfers between devices with their start and end apart: 12 -> 16, of which waited for: 8 -> 9; matrix products, arithmetic and copies ran while one was open for 4% -> 4% of each run, Pallas kernels for 0% -> 0%
where the time goes in v1:
time: 930 us; the launch traced here: 928 us
  waiting for transfers between devices  460 us (49%)
  blocking collectives  313 us (34%)
  matrix products  67.2 us (7%)
  starting transfers between devices  39 us (4%)
  between operations  22.5 us (2%)
  other arithmetic  15.8 us (2%)
  local copies, waits for them, and re-layouts  10.3 us (1%)
    unnamed x8, waiting for transfers between devices  452 us
    psum x3, blocking collectives, shards(): dual_sq = lax.psum(dual_local, ('tm', 'bat'))  313 us
    dot_general x4, matrix products, feeder_apply(): jnp.einsum('rjk,jmk->rjm', picked, block_values, precision=HIGH)  36.7 us
    all_to_all x4, starting transfers between devices, tiled_gather(): return lax.all_to_all(copies, axis, dim, dim, tiled=True)  27.2 us
    dot_general x4, matrix products, feeder_adjoint(): pushed = jnp.einsum('rjm,jmk->rjk', chosen, block_values, precision=HIGH)  23.3 us
  transfers between devices with their start and end apart: 16, of which 9 were waited for; matrix products, arithmetic and copies ran while one was open for 4% of the time, Pallas kernels for 0%

profile of v1, /device:TPU:2, one launch (start us, length us, event | category | flops | bytes accessed | tf_op | source)
XLA Modules:
  0.0 928.1 jit_solution(6738354166904598073)
XLA Ops:
  7.2 1.5 concatenate.36
  8.8 9.2 all-to-all-start
  18.0 0.7 slice.53
  18.7 1.3 collective-permute-start
  20.0 0.7 slice.52
  22.1 0.7 slice.51
  22.9 0.7 neg.3
  23.6 1.4 all-to-all-done
  25.5 5.8 convolution_bitcast_fusion.15
  32.5 1.6 collective-permute-start.1
  34.1 0.8 collective-permute-done.1
  36.0 9.2 convolution_bitcast_fusion.14
  45.6 0.7 copy.119
  46.4 1.3 dynamic-slice
  47.7 118.1 %all-reduce.12.cloned.1.call-done = f32[16,3072]{1,0:T(8,128)} async-done(((f32[16,3072]{1,0:T(8,128)}), f32[16,3072]{1,0:T(8,128)}) %all-reduce.12.cloned.1.call-update) | async-done | bytes 196624
  165.8 2.2 multiply_reduce_fusion.5
  167.9 0.8 concatenate.39
  168.7 5.8 all-to-all-start.1
  174.5 1.3 collective-permute-start.2
  177.1 105.4 %all-reduce.6 = (f32[]{:T(128)}, f32[]{:T(128)}) all-reduce(f32[]{:T(128)S(6)} %add.99, f32[]{:T(128)} %get-tuple-element.31), channel_id=1, replica_groups=mesh['tm'=32,'bat'=16] {'tm','bat'}, use_global_device_ids=true, to_apply=%region_4.5 | all-reduce | flops 2 | bytes 16 | tf_op jit(solution)/shard_map/psum | solution.py:114
  284.4 5.8 convolution_bitcast_fusion.13
  291.3 1.9 collective-permute-start.3
  295.0 9.2 convolution_bitcast_fusion.12
  304.6 0.7 copy.118
  305.4 113.0 %all-reduce.14.cloned.1.call-done = f32[16,3072]{1,0:T(8,128)} async-done(((f32[16,3072]{1,0:T(8,128)}), f32[16,3072]{1,0:T(8,128)}) %all-reduce.14.cloned.1.call-update) | async-done | bytes 196624
  418.3 2.2 multiply_reduce_fusion.4
  420.5 0.8 concatenate.42
  421.3 5.8 all-to-all-start.2
  427.1 1.3 collective-permute-start.4
  429.7 105.4 %all-reduce.5 = (f32[]{:T(128)}, f32[]{:T(128)}) all-reduce(f32[]{:T(128)S(6)} %add.106, f32[]{:T(128)} %get-tuple-element.23), channel_id=1, replica_groups=mesh['tm'=32,'bat'=16] {'tm','bat'}, use_global_device_ids=true, to_apply=%region_10.11 | all-reduce | flops 2 | bytes 16 | tf_op jit(solution)/shard_map/psum | solution.py:114
  537.0 5.8 convolution_bitcast_fusion.11
  543.9 1.7 collective-permute-start.5
  545.6 0.8 collective-permute-done.5
  547.5 9.2 convolution_bitcast_fusion.10
  557.2 0.7 copy.117
  558.0 1.3 collective-permute-start.6
  559.3 111.6 %all-reduce.16.cloned.1.call-done = f32[16,3072]{1,0:T(8,128)} async-done(((f32[16,3072]{1,0:T(8,128)}), f32[16,3072]{1,0:T(8,128)}) %all-reduce.16.cloned.1.call-update) | async-done | bytes 196624
  670.9 2.2 multiply_reduce_fusion.3
  674.4 102.2 %all-reduce.4 = (f32[]{:T(128)}, f32[]{:T(128)}) all-reduce(f32[]{:T(128)S(6)} %add.113, f32[]{:T(128)} %get-tuple-element.15), channel_id=1, replica_groups=mesh['tm'=32,'bat'=16] {'tm','bat'}, use_global_device_ids=true, to_apply=%region_16.17 | all-reduce | flops 2 | bytes 16 | tf_op jit(solution)/shard_map/psum | solution.py:114
  778.0 0.8 concatenate.45
  778.8 6.5 all-to-all-start.3
  786.0 1.3 collective-permute-start.7
  787.2 5.1 all-to-all-done.3
  792.8 5.8 convolution_bitcast_fusion.9
  800.2 9.2 convolution_bitcast_fusion.8
  809.8 0.7 copy.116
  810.6 108.8 %all-reduce.18.cloned.1.call-done = f32[16,3072]{1,0:T(8,128)} async-done(((f32[16,3072]{1,0:T(8,128)}), f32[16,3072]{1,0:T(8,128)}) %all-reduce.18.cloned.1.call-update) | async-done | bytes 196624
  919.4 2.1 fusion.92
  (79 shorter events, 14.7 us)
Async XLA Ops:
  7.2 24.6 %copy-start.2 = (f32[16,384]{1,0:T(8,128)S(1)}, f32[16,384]{1,0:T(8,128)}, u32[]{:S(2)}) copy-start(f32[16,384]{1,0:T(8,128)} %param.14) | copy-start | bytes 73732
  7.2 24.6 %copy-start.6 = (f32[384]{0:T(512)S(1)}, f32[384]{0:T(512)}, u32[]{:S(2)}) copy-start(f32[384]{0:T(512)} %param.18) | copy-start | bytes 4612
  7.2 24.6 %copy-start.4 = (f32[16,384]{1,0:T(8,128)S(1)}, f32[16,384]{1,0:T(8,128)}, u32[]{:S(2)}) copy-start(f32[16,384]{1,0:T(8,128)} %param.12) | copy-start | bytes 73732
  7.2 24.6 %copy-start.5 = (f32[16,384]{1,0:T(8,128)S(1)}, f32[16,384]{1,0:T(8,128)}, u32[]{:S(2)}) copy-start(f32[16,384]{1,0:T(8,128)} %param.13) | copy-start | bytes 73732
  7.2 24.6 %copy-start.1 = (f32[16,384]{1,0:T(8,128)S(1)}, f32[16,384]{1,0:T(8,128)}, u32[]{:S(2)}) copy-start(f32[16,384]{1,0:T(8,128)} %param.16) | copy-start | bytes 73732
  7.2 24.6 %copy-start.8 = (f32[384]{0:T(512)S(1)}, f32[384]{0:T(512)}, u32[]{:S(2)}) copy-start(f32[384]{0:T(512)} %param.19) | copy-start | bytes 4612
  7.2 27.7 %copy-start = (f32[16,384]{1,0:T(8,128)S(1)}, f32[16,384]{1,0:T(8,128)}, u32[]{:S(2)}) copy-start(f32[16,384]{1,0:T(8,128)} %param.17) | copy-start | bytes 73732
  8.8 16.3 %all-to-all-start = ((f32[16,1,3072]{2,1,0:T(1,128)}), f32[16,1,3072]{2,1,0:T(1,128)S(1)}, u32[]{:S(2)}, u32[]{:S(2)}) async-start(f32[16,1,3072]{2,1,0:T(1,128)} %concatenate.36), calls=%async_computation | async-start | bytes 393216 | tf_op jit(solution)/shard_map/all_to_all | solution.py:14
  18.0 147.8 %all-reduce.12.cloned.1.call-start = ((), (), s32[]{:S(2)}) async-start(), calls=%async_computation.4 | async-start | bytes 393216
  18.7 13.1 %collective-permute-start = (f32[1,384]{1,0:T(1,128)S(1)}, f32[1,384]{1,0:T(1,128)S(1)}, u32[]{:S(2)}, u32[]{:S(2)}) collective-permute-start(f32[1,384]{1,0:T(1,128)S(1)} %slice.53), channel_id=1, source_target_pairs={{16,0},{32,16},{48,32},{64,48},{80,64},{96,80},{112,96},{128,112},... | collective-permute-start | bytes 4616 | tf_op jit(solution)/shard_map/ppermute | solution.py:20
  31.3 134.4 %copy-start.3 = (f32[3072]{0:T(1024)S(1)}, f32[3072]{0:T(1024)}, u32[]{:S(2)}) copy-start(f32[3072]{0:T(1024)} %param.20) | copy-start | bytes 36868
  31.3 134.4 %copy-start.7 = (f32[1,3072]{1,0:T(1,128)S(1)}, f32[1,3072]{1,0:T(1,128)}, u32[]{:S(2)}) copy-start(f32[1,3072]{1,0:T(1,128)} %param.15) | copy-start | bytes 36868
  32.5 2.4 collective-permute-start.1
  168.7 115.3 %all-to-all-start.1 = ((f32[16,1,3072]{2,1,0:T(1,128)}), f32[16,1,3072]{2,1,0:T(1,128)S(1)}, u32[]{:S(2)}, u32[]{:S(2)}) async-start(f32[16,1,3072]{2,1,0:T(1,128)} %concatenate.39), calls=%async_computation.1 | async-start | bytes 393216 | tf_op jit(solution)/shard_map/all_to_all | solution.py:14
  174.5 243.9 %all-reduce.14.cloned.1.call-start = ((), (), s32[]{:S(2)}) async-start(), calls=%async_computation.5 | async-start | bytes 393216
  174.5 116.2 %collective-permute-start.2 = (f32[1,384]{1,0:T(1,128)S(1)}, f32[1,384]{1,0:T(1,128)S(1)}, u32[]{:S(2)}, u32[]{:S(2)}) collective-permute-start(f32[1,384]{1,0:T(1,128)S(1)} %slice.71), channel_id=1, source_target_pairs={{16,0},{32,16},{48,32},{64,48},{80,64},{96,80},{112,96},{128,112},... | collective-permute-start | bytes 4616 | tf_op jit(solution)/shard_map/ppermute | solution.py:20
  291.3 2.5 collective-permute-start.3
  421.3 115.3 %all-to-all-start.2 = ((f32[16,1,3072]{2,1,0:T(1,128)}), f32[16,1,3072]{2,1,0:T(1,128)S(1)}, u32[]{:S(2)}, u32[]{:S(2)}) async-start(f32[16,1,3072]{2,1,0:T(1,128)} %concatenate.42), calls=%async_computation.2 | async-start | bytes 393216 | tf_op jit(solution)/shard_map/all_to_all | solution.py:14
  427.0 243.9 %all-reduce.16.cloned.1.call-start = ((), (), s32[]{:S(2)}) async-start(), calls=%async_computation.6 | async-start | bytes 393216
  427.1 116.2 %collective-permute-start.4 = (f32[1,384]{1,0:T(1,128)S(1)}, f32[1,384]{1,0:T(1,128)S(1)}, u32[]{:S(2)}, u32[]{:S(2)}) collective-permute-start(f32[1,384]{1,0:T(1,128)S(1)} %slice.75), channel_id=1, source_target_pairs={{16,0},{32,16},{48,32},{64,48},{80,64},{96,80},{112,96},{128,112},... | collective-permute-start | bytes 4616 | tf_op jit(solution)/shard_map/ppermute | solution.py:20
  543.9 2.5 collective-permute-start.5
  558.0 227.4 %collective-permute-start.6 = (f32[1,384]{1,0:T(1,128)S(1)}, f32[1,384]{1,0:T(1,128)S(1)}, u32[]{:S(2)}, u32[]{:S(2)}) collective-permute-start(f32[1,384]{1,0:T(1,128)S(1)} %slice.79), channel_id=1, source_target_pairs={{16,0},{32,16},{48,32},{64,48},{80,64},{96,80},{112,96},{128,112},... | collective-permute-start | bytes 4616 | tf_op jit(solution)/shard_map/ppermute | solution.py:20
  778.8 13.5 %all-to-all-start.3 = ((f32[16,1,3072]{2,1,0:T(1,128)}), f32[16,1,3072]{2,1,0:T(1,128)S(1)}, u32[]{:S(2)}, u32[]{:S(2)}) async-start(f32[16,1,3072]{2,1,0:T(1,128)} %concatenate.45), calls=%async_computation.3 | async-start | bytes 393216 | tf_op jit(solution)/shard_map/all_to_all | solution.py:14
  785.3 134.1 %all-reduce.18.cloned.1.call-start = ((), (), s32[]{:S(2)}) async-start(), calls=%async_computation.7 | async-start | bytes 393216
  786.0 13.1 %collective-permute-start.7 = (f32[1,384]{1,0:T(1,128)S(1)}, f32[1,384]{1,0:T(1,128)S(1)}, u32[]{:S(2)}, u32[]{:S(2)}) collective-permute-start(f32[1,384]{1,0:T(1,128)S(1)} %slice.80), channel_id=1, source_target_pairs={{0,16},{16,32},{32,48},{48,64},{64,80},{80,96},{96,112},{112,128},... | collective-permute-start | bytes 4616 | tf_op jit(solution)/shard_map/ppermute | solution.py:20
Sparse Core Ops, SparseCore 0:
  46.5 119.2 all-reduce.11
  305.5 112.8 all-reduce.13
  558.1 112.8 all-reduce.15
  810.7 108.6 all-reduce.17
